TPU v7x, 32 devices: a whole 2x2x4 slice. The times are simulated.
32 devices in a mesh: band: 8 (over z, x), quarter: 4 (over y, core).
Axes of the slice: x: 2, y: 2, z: 4, core: 2. Of those that a mesh axis runs over, the one named last changes fastest.
Arguments:
- voltages: bfloat16 [32, 2, 524288], P('band', None, 'quarter'), may hold values from -6 to 6
- flagged: int32 [32], P('band'), may hold values 0 or 1
- antenna_source_lookup: int32 [32], replicated, may hold values from 0 to 31, each once
Outputs:
- visibility: bfloat16 [2, 16, 64, 64], P(None, 'band', 'quarter')
Inputs may be any that keep to these rules, and one draw needn't show every extreme that they name: `antenna_source_lookup`: every input antenna appears exactly once.
All inputs are finite; a program needn't handle non-finite values. No bound on the sum of `flagged` on one device may be relied on, other than what follows from the above.
Results may differ from a plain program's by a relative error of at most 0.0074.
Values may be sent and summed in bfloat16 or wider, within the bound.
A program may use at most 64 MiB of HBM per device.

v0:
```python
import math

import jax
import jax.numpy as jnp
from jax import lax
from jax.sharding import PartitionSpec as P

FRAME = 8192
TAPS = 4
CH_DEV = 2


def passed_along(shard, axis, by):
    count = lax.axis_size(axis)
    pairs = [(i, i + by) for i in range(count) if 0 <= i + by < count]
    return lax.ppermute(shard, axis, pairs)


def pfb_window():
    sample_pos = jnp.arange(TAPS * FRAME, dtype=jnp.float32) + 0.5
    offset_units = sample_pos / FRAME - TAPS / 2.0
    hann_taper = 0.5 - 0.5 * jnp.cos(sample_pos * (2.0 * math.pi / (TAPS * FRAME)))
    return (jnp.sinc(offset_units) * hann_taper).reshape(TAPS, FRAME)


def dft_rows(channels):
    bins = jnp.arange(channels, dtype=jnp.int32) + FRAME // 8
    sample_index = jnp.arange(FRAME, dtype=jnp.int32)
    phase_steps = bins[:, None] * sample_index[None, :] % FRAME
    angles = phase_steps.astype(jnp.float32) * (2.0 * math.pi / FRAME)
    stacked = jnp.stack([jnp.cos(angles), -jnp.sin(angles)], axis=1)
    return stacked.reshape(2 * channels, FRAME).astype(jnp.bfloat16)


def left_side(own_rows):
    real_part = own_rows[:, 0]
    imag_part = own_rows[:, 1]
    first = jnp.concatenate([real_part, imag_part], axis=1)
    second = jnp.concatenate([imag_part, -real_part], axis=1)
    return jnp.stack([first, second], axis=1)


def pair_product(left_rows, other_rows):
    right_side = jnp.concatenate([other_rows[:, 0], other_rows[:, 1]], axis=1)
    return jnp.einsum("coki,ckj->ocij", left_rows, right_side, preferred_element_type=jnp.float32)


def table_product(table_rows, windowed_rows):
    return lax.dot_general(
        table_rows, windowed_rows, (((1,), (1,)), ((), ())), preferred_element_type=jnp.float32
    )


def shards(voltages, flagged, antenna_source_lookup):
    antenna_per_device, polarization_count, device_local_samples = voltages.shape
    band_count = lax.axis_size("band")
    quarters = lax.axis_size("quarter")
    spec_dev = device_local_samples // FRAME
    device_signals = antenna_per_device * polarization_count
    keep_mask = (1 - flagged).astype(jnp.bfloat16)
    frames = (voltages * keep_mask[:, None, None]).reshape(device_signals, spec_dev, FRAME)
    window = pfb_window()
    channels = CH_DEV * band_count
    dft_table = dft_rows(channels)
    edge = TAPS - 1
    following = passed_along(frames[:, :edge], "quarter", -1)
    extended = jnp.concatenate([frames, following], axis=1)
    columns = device_signals * spec_dev
    tap_rows = []
    for tap_index in range(TAPS):
        tap_win = (
            window[tap_index] * extended[:, tap_index : tap_index + spec_dev].astype(jnp.float32)
        ).astype(jnp.bfloat16)
        tap_rows.append(tap_win.reshape(columns, FRAME))
    inv_root = 1.0 / math.sqrt(FRAME)
    result = table_product(dft_table, tap_rows[0])
    for tap_index in range(1, TAPS):
        result = result + table_product(dft_table, tap_rows[tap_index])
    turned = lax.all_to_all(
        (result * inv_root).astype(jnp.bfloat16).reshape(band_count, CH_DEV, 2, columns),
        "band",
        split_axis=0,
        concat_axis=0,
        tiled=True,
    )
    channel_major = turned.reshape(band_count, CH_DEV, 2, device_signals, spec_dev)
    channel_major = channel_major.transpose(1, 2, 4, 0, 3).reshape(
        CH_DEV, 2, spec_dev, band_count * device_signals
    )
    signal_index = (
        antenna_source_lookup[:, None] * polarization_count
        + jnp.arange(polarization_count, dtype=jnp.int32)[None, :]
    ).reshape(-1)
    channel_major = jnp.take(channel_major, signal_index, axis=3)
    total_sig = channel_major.shape[3]
    quarter_rows = total_sig // quarters
    start_row = lax.axis_index("quarter") * quarter_rows
    shard_piece = lax.all_gather(channel_major, "quarter", axis=2, tiled=True)
    own_rows = lax.dynamic_slice_in_dim(shard_piece, start_row, quarter_rows, 3)
    visibility = pair_product(left_side(own_rows), shard_piece)
    return (visibility * (1.0 / (spec_dev * quarters))).astype(jnp.bfloat16)


def solution(mesh):
    placed = (P("band", None, "quarter"), P("band"), P())
    return jax.shard_map(
        shards,
        mesh=mesh,
        in_specs=placed,
        out_specs=P(None, "band", "quarter", None),
        check_vma=False,
    )
```

profile of v0, /device:TPU:0, one launch (start us, length us, event | category | flops | bytes accessed | tf_op | source)
XLA Modules:
  0.0 57.7 jit_solution(4234828040600836542)
XLA Ops:
  0.0 0.6 %fusion.13 = f32[32768]{0:T(1024)S(1)} fusion(), kind=kLoop, calls=%fused_computation.34 | loop fusion | flops 1310720 | bytes 131072 | tf_op jit(solution)/shard_map/mul | solution.py:23
  0.6 0.7 %subtract_convert_fusion = bf16[4]{0:T(256)(128)(2,1)S(1)} fusion(s32[4]{0:T(128)} %param.4), kind=kLoop, calls=%fused_computation.67 | loop fusion | flops 8 | bytes 24 | tf_op jit(solution)/shard_map/convert_element_type | solution.py:60
  1.4 0.1 copy.41
  1.5 6.5 %multiply_convert_fusion.3 = (bf16[4,2,131072]{2,1,0:T(2,128)(2,1)}, bf16[4,2,131072]{2,1,0:T(2,128)(2,1)}) fusion(f32[131072]{0:T(1024)S(1)} %bitcast.47, bf16[4,2,131072]{2,1,0:T(2,128)(2,1)} %param.3, bf16[4]{0:T(256)(128)(2,1)S(1)} %subtract_convert_fusion), kind=kLoop, calls=%fused_computation.4 | loop fusion | flops 4194304 | bytes 6815752 | tf_op jit(solution)/shard_map/convert_element_type | solution.py:73
  8.0 0.0 copy-start.2
  8.0 3.6 %reshape.200 = bf16[8,16,8192]{2,1,0:T(8,128)(2,1)S(1)} reshape(bf16[4,2,131072]{2,1,0:T(2,128)(2,1)} %get-tuple-element.6) | data formatting | bytes 4194304 | tf_op jit(solution)/shard_map/reshape | solution.py:61
  11.5 0.0 copy-start.1
  11.6 1.1 %slice.56 = bf16[8,3,8192]{2,1,0:T(4,128)(2,1)} slice(bf16[8,16,8192]{2,1,0:T(8,128)(2,1)S(1)} %reshape.200), slice={[0:8], [0:3], [0:8192]} | slice | bytes 786432 | tf_op jit(solution)/shard_map/slice | solution.py:66
  12.7 1.3 %collective-permute-start = (bf16[8,3,8192]{2,1,0:T(4,128)(2,1)}, bf16[8,3,8192]{2,1,0:T(4,128)(2,1)}, u32[]{:S(2)}, u32[]{:S(2)}) collective-permute-start(bf16[8,3,8192]{2,1,0:T(4,128)(2,1)} %slice.56), channel_id=1, source_target_pairs={{1,0},{2,1},{3,2},{5,4},{6,5},{7,6},{9,8},{10,9},{11,10},{13,12},{... | collective-permute-start | bytes 1179656 | tf_op jit(solution)/shard_map/ppermute | solution.py:16
  14.0 0.0 copy-done.2
  14.0 0.1 iota_add_fusion
  14.1 0.1 add.219
  14.2 0.0 copy-done.1
  14.2 0.1 add.197
  14.3 1.7 %constant_dynamic-update-slice_fusion.1 = bf16[8,19,8192]{2,1,0:T(8,128)(2,1)S(1)} fusion(bf16[8,16,8192]{2,1,0:T(8,128)(2,1)} %copy-done.1), kind=kLoop, calls=%fused_computation.62 | loop fusion | bytes 4194304
  16.1 2.5 %cosine_convert_fusion = (bf16[16,1,8192]{2,0,1:T(8,128)(2,1)S(1)}, bf16[16,1,8192]{2,0,1:T(8,128)(2,1)S(1)}) fusion(s32[16]{0:T(128)S(1)} %iota_add_fusion.1), kind=kLoop, calls=%fused_computation.19 | loop fusion | flops 2228224 | bytes 524352 | tf_op jit(solution)/shard_map/convert
  18.5 0.1 pad_maximum_fusion
  18.6 1.4 %copy.27 = bf16[16,2,8192]{2,1,0:T(2,128)(2,1)} copy(bf16[16,2,8192]{2,0,1:T(8,128)(2,1)S(1)} %pad_maximum_fusion) | data formatting | bytes 1048576 | tf_op jit(solution)/shard_map/stack | solution.py:31
  20.0 2.1 %convert_element_type.86 = bf16[32,8192]{1,0:T(8,128)(2,1)} reshape(bf16[16,2,8192]{2,1,0:T(2,128)(2,1)} %copy.27) | data formatting | bytes 1048576 | tf_op jit(solution)/shard_map/convert_element_type | solution.py:32
  22.0 4.7 %convert_element_type.90 = bf16[128,8192]{1,0:T(8,128)(2,1)} reshape(bf16[4,2,131072]{2,1,0:T(2,128)(2,1)} %get-tuple-element.5) | data formatting | bytes 4194304 | tf_op jit(solution)/shard_map/convert_element_type | solution.py:73
  26.7 2.6 %fusion.32 = f32[32,128]{1,0:T(8,128)S(1)} fusion(bf16[32,8192]{1,0:T(8,128)(2,1)} %convert_element_type.86, bf16[128,8192]{1,0:T(8,128)(2,1)} %convert_element_type.90), kind=kOutput, calls=%fused_computation.76 | convolution fusion | flops 67108864 | bytes 2637824 | tf_op jit(solution)/shard_map/dot_general | solution.py:49
  29.3 0.0 collective-permute-done
  29.3 1.4 %constant_dynamic-update-slice_fusion = bf16[8,19,8192]{2,1,0:T(8,128)(2,1)S(1)} fusion(bf16[8,19,8192]{2,1,0:T(8,128)(2,1)S(1)} %constant_dynamic-update-slice_fusion.1, bf16[8,3,8192]{2,1,0:T(4,128)(2,1)} %collective-permute-done), kind=kLoop, calls=%fused_computation.61 | loop fusion | bytes 917504 | tf_op jit(solution)/shard_map/concatenate | solution.py:67
  30.7 0.0 copy-start
  30.7 1.8 %multiply_convert_fusion.1 = (bf16[8,16,8192]{2,1,0:T(8,128)(2,1)S(1)}, bf16[8,16,8192]{2,1,0:T(8,128)(2,1)S(1)}, bf16[8,16,8192]{2,1,0:T(8,128)(2,1)S(1)}) fusion(bf16[8,19,8192]{2,1,0:T(8,128)(2,1)S(1)} %constant_dynamic-update-slice_fusion, f32[8192]{0:T(1024)S(1)} %get-tuple-element.10, f32[8192]{0:T(1024)S(1)} %get-tuple-element.11, ...), kind=kLoop, calls=%fused_computation.2 | loop fusion | flops 9437184 | bytes 12681216 | tf_op jit(solution)/shard_map/convert_element_type | solution.py:73
  32.5 0.0 copy-done
  32.5 0.8 %fusion.33 = f32[32,128]{1,0:T(8,128)S(1)} fusion(bf16[32,8192]{1,0:T(8,128)(2,1)S(1)} %copy-done, bf16[128,8192]{1,0:T(8,128)(2,1)S(1)} %bitcast.44), kind=kOutput, calls=%fused_computation.77 | convolution fusion | flops 67108864 | bytes 2637824 | tf_op jit(solution)/shard_map/dot_general | solution.py:49
  33.3 0.8 %convolution_add_fusion.1 = f32[32,128]{1,0:T(8,128)S(1)} fusion(f32[32,128]{1,0:T(8,128)S(1)} %fusion.32, bf16[32,8192]{1,0:T(8,128)(2,1)S(1)} %copy-done, bf16[128,8192]{1,0:T(8,128)(2,1)S(1)} %bitcast.46), kind=kOutput, calls=%fused_computation.8 | convolution fusion | flops 67112960 | bytes 2654208 | tf_op jit(solution)/shard_map/dot_general | solution.py:49
  34.2 1.4 %fusion.2 = bf16[32,128]{1,0:T(8,128)(2,1)} fusion(f32[32,128]{1,0:T(8,128)S(1)} %fusion.33, f32[32,128]{1,0:T(8,128)S(1)} %convolution_add_fusion.1, bf16[32,8192]{1,0:T(8,128)(2,1)S(1)} %copy-done, bf16[128,8192]{1,0:T(8,128)(2,1)S(1)} %bitcast.45), kind=kOutput, calls=%fused_computation.9 | convolution fusion | flops 67125248 | bytes 2662400 | tf_op jit(solution)/shard_map/dot_general | solution.py:49
  35.6 7.3 %all-to-all-start = ((bf16[8,2,2,128]{3,2,1,0:T(2,128)(2,1)}), bf16[8,2,2,128]{3,2,1,0:T(2,128)(2,1)S(1)}, u32[]{:S(2)}, u32[]{:S(2)}) async-start(bf16[8,2,2,128]{3,2,1,0:T(2,128)(2,1)} %bitcast.3), calls=%async_computation | async-start | bytes 16384 | tf_op jit(solution)/shard_map/all_to_all | solution.py:79
  42.9 6.5 %all-to-all-done = bf16[8,2,2,128]{3,2,1,0:T(2,128)(2,1)S(1)} async-done(((bf16[8,2,2,128]{3,2,1,0:T(2,128)(2,1)}), bf16[8,2,2,128]{3,2,1,0:T(2,128)(2,1)S(1)}, u32[]{:S(2)}, u32[]{:S(2)}) %all-to-all-start) | async-done | bytes 8224 | tf_op jit(solution)/shard_map/all_to_all | solution.py:79
  49.4 0.1 reshape.205
  49.5 0.1 copy.29
  49.6 0.7 %gather_fusion = bf16[64,2,2,16]{3,2,1,0:T(2,128)(2,1)S(1)} fusion(bf16[2,2,16,64]{2,1,3,0:T(2,128)(2,1)S(1)} %copy.29, s32[1024]{0:T(1024)S(1)} %pad_clamp_fusion), kind=kCustom, calls=%fused_computation | custom fusion | bytes 16640 | tf_op jit(solution)/shard_map/jit(_take)/gather | solution.py:94
  50.3 0.1 fusion.22
  50.5 0.1 copy.30
  50.6 5.5 %all_gather.3 = bf16[2,2,64,64]{3,1,0,2:T(2,128)(2,1)S(1)} all-gather(bf16[2,2,16,64]{3,1,0,2:T(2,128)(2,1)S(1)} %copy.30), channel_id=1, replica_groups=mesh['band'=8,'quarter'=4] {'quarter'}, dimensions={2}, use_global_device_ids=true | all-gather | bytes 40960 | tf_op jit(solution)/shard_map/all_gather | solution.py:98
  56.1 0.1 fusion.31
  56.2 0.2 constant_dynamic-slice_fusion.1
  56.4 0.1 copy.40
  56.5 0.1 copy.39
  56.6 0.1 copy.36
  56.7 0.1 copy.37
  56.8 0.1 maximum_bitcast_fusion
  56.9 0.2 fusion.23
  57.1 0.6 %copy.35 = bf16[2,2,16,64]{3,2,1,0:T(8,128)(2,1)} copy(bf16[2,2,16,64]{3,2,0,1:T(8,128)(2,1)S(1)} %fusion.27) | data formatting | bytes 16384 | tf_op jit(solution)/shard_map/convert_element_type | solution.py:101
  (11 shorter events, 0.1 us)
Async XLA Ops:
  8.0 6.0 %copy-start.2 = (s32[32]{0:T(128)S(1)}, s32[32]{0:T(128)}, u32[]{:S(2)}) copy-start(s32[32]{0:T(128)} %param.5) | copy-start | bytes 388
  11.5 2.6 %copy-start.1 = (bf16[8,16,8192]{2,1,0:T(8,128)(2,1)}, bf16[8,16,8192]{2,1,0:T(8,128)(2,1)S(1)}, u32[]{:S(2)}) copy-start(bf16[8,16,8192]{2,1,0:T(8,128)(2,1)S(1)} %reshape.200) | copy-start | bytes 6291460
  12.7 16.6 %collective-permute-start = (bf16[8,3,8192]{2,1,0:T(4,128)(2,1)}, bf16[8,3,8192]{2,1,0:T(4,128)(2,1)}, u32[]{:S(2)}, u32[]{:S(2)}) collective-permute-start(bf16[8,3,8192]{2,1,0:T(4,128)(2,1)} %slice.56), channel_id=1, source_target_pairs={{1,0},{2,1},{3,2},{5,4},{6,5},{7,6},{9,8},{10,9},{11,10},{13,12},{... | collective-permute-start | bytes 1179656 | tf_op jit(solution)/shard_map/ppermute | solution.py:16
  30.7 1.8 %copy-start = (bf16[32,8192]{1,0:T(8,128)(2,1)S(1)}, bf16[32,8192]{1,0:T(8,128)(2,1)}, u32[]{:S(2)}) copy-start(bf16[32,8192]{1,0:T(8,128)(2,1)} %convert_element_type.86) | copy-start | bytes 1572868
  35.6 13.8 %all-to-all-start = ((bf16[8,2,2,128]{3,2,1,0:T(2,128)(2,1)}), bf16[8,2,2,128]{3,2,1,0:T(2,128)(2,1)S(1)}, u32[]{:S(2)}, u32[]{:S(2)}) async-start(bf16[8,2,2,128]{3,2,1,0:T(2,128)(2,1)} %bitcast.3), calls=%async_computation | async-start | bytes 16384 | tf_op jit(solution)/shard_map/all_to_all | solution.py:79
where the time goes:
time: 58.2 us; the launch traced here: 57.7 us
  local copies, waits for them, and re-layouts  18.6 us (32%)
  other arithmetic  12.5 us (21%)
  starting transfers between devices  8.56 us (15%)
  waiting for transfers between devices  6.53 us (11%)
  matrix products  5.84 us (10%)
  blocking collectives  5.48 us (9%)
    convert_element_type x2, other arithmetic, shards(): tap_win = (window[tap_index] * extended[:, tap_index:tap_index + spec_dev...  8.3 us
    all_to_all x1, starting transfers between devices, shards(): lax.all_to_all((result * inv_root).astype(jnp.bfloat16).reshape(band_coun...  7.28 us
    all_to_all x1, waiting for transfers between devices, shards(): lax.all_to_all((result * inv_root).astype(jnp.bfloat16).reshape(band_coun...  6.51 us
    dot_general x4, matrix products, table_product(): lax.dot_general(table_rows, windowed_rows, (((1,), (1,)), ((), ())), pref...  5.63 us
    all_gather x1, blocking collectives, shards(): shard_piece = lax.all_gather(channel_major, 'quarter', axis=2, tiled=True)  5.48 us
    convert_element_type x1, local copies, waits for them, and re-layouts, shards(): tap_win = (window[tap_index] * extended[:, tap_index:tap_index + spec_dev...  4.67 us
    reshape x1, local copies, waits for them, and re-layouts, shards(): (voltages * keep_mask[:, None, None]).reshape(device_signals, spec_dev, F...  3.58 us
    another operation x1, other arithmetic  2.47 us
  transfers between devices with their start and end apart: 2, of which 1 were waited for; matrix products, arithmetic and copies ran while one was open for 26% of the time, Pallas kernels for 0%

commit v1 on v0

v1 whole, which is shorter than its diff:
```python
import functools
import math

import jax
import jax.numpy as jnp
import ml_dtypes
import numpy as np
from jax import lax
from jax.experimental import pallas as pl
from jax.experimental.pallas import tpu as pltpu
from jax.sharding import PartitionSpec as P

FRAME = 8192
TAPS = 4
CH_DEV = 2
LANES = 128
CHUNKS = 8
MESH = pl.DeviceIdType.MESH


def weights(bands):
    pos = np.arange(TAPS * FRAME) + 0.5
    window = np.sinc(pos / FRAME - TAPS / 2) * (0.5 - 0.5 * np.cos(2 * np.pi * pos / (TAPS * FRAME)))
    window = window.reshape(TAPS, FRAME)
    band = np.arange(bands)[None, :]
    channel = np.arange(CH_DEV)[:, None]
    bins = band * CH_DEV + channel + FRAME // 8
    phase = bins[:, :, None] * np.arange(FRAME) % FRAME
    angle = phase * (2 * np.pi / FRAME)
    table = np.stack([np.cos(angle), -np.sin(angle)], axis=1) / math.sqrt(FRAME)
    table = table.reshape(1, 2 * CH_DEV * bands, FRAME)
    both = (window[:, None, :] * table).reshape(TAPS * 2 * CH_DEV * bands, CHUNKS, FRAME // CHUNKS)
    return np.ascontiguousarray(both.transpose(1, 0, 2)).astype(ml_dtypes.bfloat16)


def kernel(bands, quarters, ants, pols, spec, flag_ref, look_ref, x_ref, w_ref, out_ref,
           xb, wb, xf, sf, send, recv, rf, x_sem, w_sem, own_sem, send_sem, recv_sem):
    count = bands * quarters
    parts = 2 * CH_DEV
    my_band, my_quarter = lax.axis_index("band"), lax.axis_index("quarter")
    me = my_quarter * bands + my_band
    wide = xb.shape[2] // pols

    def x_copy(g):
        return pltpu.make_async_copy(x_ref.at[:, pl.ds(g * pols * wide, pols * wide), :], xb.at[g], x_sem.at[g])

    def w_copy(g):
        return pltpu.make_async_copy(w_ref.at[g], wb.at[g], w_sem.at[g])

    for g in range(CHUNKS):
        x_copy(g).start()
        w_copy(g).start()

    barrier = pltpu.get_barrier_semaphore()

    def device(k):
        d = lax.rem(me + k, count)
        return d, lax.rem(d, bands), lax.div(d, bands)

    @pl.loop(1, count)
    def _(k):
        _, b, q = device(k)
        pl.semaphore_signal(barrier, inc=1, device_id=(b, q), device_id_type=MESH)

    acc = None
    rows = x_ref.shape[0]
    for g in range(CHUNKS):
        x_copy(g).wait()
        w_copy(g).wait()
        xf[...] = xb[g].astype(jnp.float32).reshape(rows * pols * wide, LANES)
        pieces = []
        for j in range(wide):
            pieces.append(jnp.concatenate(
                [xf[pl.ds(pols * j + p, rows, stride=pols * wide), :] for p in range(pols)], axis=0
            ).astype(jnp.bfloat16))
        block = jnp.concatenate(pieces, axis=1)
        part = lax.dot_general(wb[g], block, (((1,), (1,)), ((), ())), preferred_element_type=jnp.float32)
        acc = part if acc is None else acc + part

    group = parts * bands
    columns = pols * rows
    lane = lax.broadcasted_iota(jnp.int32, (1, columns), 1)
    spot = lane % spec
    ant = (lane // spec) % ants
    keep = jnp.zeros((1, columns), jnp.float32)
    for a in range(ants):
        keep = jnp.where(ant == a, (1 - flag_ref[a]).astype(jnp.float32), keep)
    main = acc[:group]
    halo = jnp.zeros_like(main)
    for t in range(1, TAPS):
        moved = pltpu.roll(acc[t * group:(t + 1) * group], columns - t, 1)
        inside = spot + t < spec
        main = main + jnp.where(inside, moved, 0.0)
        halo = halo + jnp.where(inside, 0.0, moved)
    main = main * keep
    halo = pltpu.roll(halo, spec, 1) * keep
    for k in range(parts):
        sf[pl.ds(k, bands, stride=2 * parts), :] = main[k * bands:(k + 1) * bands]
        sf[pl.ds(parts + k, bands, stride=2 * parts), :] = halo[k * bands:(k + 1) * bands]
    send[...] = sf[...].reshape(bands, 2 * parts, columns).astype(jnp.bfloat16)

    pl.semaphore_wait(barrier, count - 1)

    def remote(k):
        _, b, q = device(k)
        return pltpu.make_async_remote_copy(
            src_ref=send.at[b], dst_ref=recv.at[me], send_sem=send_sem.at[k], recv_sem=recv_sem.at[me],
            device_id=(b, q), device_id_type=MESH)

    @pl.loop(1, count)
    def _(k):
        remote(k).start()

    own = pltpu.make_async_copy(send.at[my_band], recv.at[me], own_sem)
    own.start()

    signals = bands * ants * pols
    antennas = bands * ants
    look = look_ref[...].astype(jnp.float32)
    out_rows = signals // quarters

    def chooser(first, size):
        g = first + lax.broadcasted_iota(jnp.int32, (size, antennas), 0)
        i = lax.broadcasted_iota(jnp.int32, (size, antennas), 1)
        source = jnp.sum(jnp.where(i == g // pols, look, 0.0), axis=1, keepdims=True)
        g = first + lax.broadcasted_iota(jnp.int32, (size, signals), 0)
        row = lax.broadcasted_iota(jnp.int32, (size, signals), 1)
        kind = row // bands
        antenna = ((row % bands) * ants + kind % ants).astype(jnp.float32)
        hit = jnp.logical_and(antenna == source, g % pols == kind // ants)
        return jnp.where(hit, 1.0, 0.0).astype(jnp.bfloat16)

    all_rows = chooser(0, signals)
    own_rows = chooser(my_quarter * out_rows, out_rows)

    own.wait()

    @pl.loop(1, count)
    def _(k):
        remote(k).wait_send()
        d, b, q = device(k)
        pltpu.make_async_remote_copy(
            src_ref=send.at[b], dst_ref=recv.at[d], send_sem=send_sem.at[k], recv_sem=recv_sem.at[d],
            device_id=(b, q), device_id_type=MESH).wait_recv()

    rf[...] = recv[...].astype(jnp.float32).reshape(count * 2 * parts, columns)

    def rows_of(q, k):
        return rf[pl.ds(q * bands * 2 * parts + k, bands, stride=2 * parts), :]

    flipped = lax.broadcasted_iota(jnp.int32, (1, columns), 1)
    scale = 1.0 / (spec * quarters)
    for c in range(CH_DEV):
        blocks = []
        for r in range(2):
            for q in range(quarters):
                full = rows_of(q, 2 * c + r)
                if q + 1 < quarters:
                    full = full + rows_of(q + 1, parts + 2 * c + r)
                blocks.append(full.astype(jnp.bfloat16).astype(jnp.float32))
        bands_of = []
        for s in range(ants * pols):
            turned = None
            for at, block in enumerate(blocks):
                by = (spec * (at - s)) % columns
                moved = pltpu.roll(block, by, 1) if by else block
                turned = moved if turned is None else jnp.where(lane // spec == at, moved, turned)
            bands_of.append(turned)
        got = jnp.concatenate(bands_of, axis=0).astype(jnp.bfloat16)
        right = jnp.dot(all_rows, got, preferred_element_type=jnp.float32).astype(jnp.bfloat16)
        left = jnp.dot(own_rows, got, preferred_element_type=jnp.float32)
        other = pltpu.roll(left, columns // 2, 1)
        other = jnp.where(flipped < columns // 2, other, -other).astype(jnp.bfloat16)
        for o, side in enumerate((left.astype(jnp.bfloat16), other)):
            product = lax.dot_general(side, right, (((1,), (1,)), ((), ())), preferred_element_type=jnp.float32)
            out_ref[o, c] = (product * scale).astype(jnp.bfloat16)


def shards(table, bands, quarters, voltages, flagged, lookup):
    ants, pols, samples = voltages.shape
    spec = samples // FRAME
    steps = FRAME // LANES
    rows = ants * spec
    columns = pols * rows
    x = voltages.reshape(ants, pols, samples // LANES, LANES).transpose(0, 2, 1, 3).reshape(rows, steps * pols, LANES)
    signals = bands * ants * pols
    parts = 2 * CH_DEV
    count = bands * quarters
    group = TAPS * parts * bands
    return pl.pallas_call(
        functools.partial(kernel, bands, quarters, ants, pols, spec),
        out_shape=jax.ShapeDtypeStruct((2, CH_DEV, signals // quarters, signals), jnp.bfloat16),
        in_specs=[
            pl.BlockSpec(memory_space=pltpu.SMEM),
            pl.BlockSpec(memory_space=pltpu.VMEM),
            pl.BlockSpec(memory_space=pl.ANY),
            pl.BlockSpec(memory_space=pl.ANY),
        ],
        out_specs=pl.BlockSpec(memory_space=pltpu.VMEM),
        scratch_shapes=[
            pltpu.VMEM((CHUNKS, rows, steps * pols // CHUNKS, LANES), jnp.bfloat16),
            pltpu.VMEM((CHUNKS, group, FRAME // CHUNKS), jnp.bfloat16),
            pltpu.VMEM((rows * steps * pols // CHUNKS, LANES), jnp.float32),
            pltpu.VMEM((bands * 2 * parts, columns), jnp.float32),
            pltpu.VMEM((bands, 2 * parts, columns), jnp.bfloat16),
            pltpu.VMEM((count, 2 * parts, columns), jnp.bfloat16),
            pltpu.VMEM((count * 2 * parts, columns), jnp.float32),
            pltpu.SemaphoreType.DMA((CHUNKS,)),
            pltpu.SemaphoreType.DMA((CHUNKS,)),
            pltpu.SemaphoreType.DMA,
            pltpu.SemaphoreType.DMA((count,)),
            pltpu.SemaphoreType.DMA((count,)),
        ],
        compiler_params=pltpu.CompilerParams(
            collective_id=0, has_side_effects=True, vmem_limit_bytes=63 * 1024 * 1024),
    )(flagged, lookup.reshape(1, -1), x, jnp.asarray(table))


def solution(mesh):
    bands, quarters = mesh.shape["band"], mesh.shape["quarter"]
    return jax.shard_map(
        functools.partial(shards, weights(bands), bands, quarters),
        mesh=mesh,
        in_specs=(P("band", None, "quarter"), P("band"), P()),
        out_specs=P(None, "band", "quarter", None),
        check_vma=False,
    )
```

time: 58.2 us -> 16.7 us (0.29)
  local copies, waits for them, and re-layouts: 18.6 us -> 1.32 us
  Pallas kernels: 0 us -> 15.1 us
  other arithmetic: 12.5 us -> 0 us
  starting transfers between devices: 8.56 us -> 0 us
  waiting for transfers between devices: 6.53 us -> 0 us
  matrix products: 5.84 us -> 0 us
  blocking collectives: 5.48 us -> 0 us
    pallas_call x0 -> x1, Pallas kernels: none -> 15.1 us  [shards(): pl.pallas_call(functools.partial(kernel, bands, quarters, ants, pols, spe...]
    convert_element_type x4 -> x0, other arithmetic: 8.98 us -> none  [the longest x2 8.3 us: shards(): tap_win = (window[tap_index] * extended[:, tap_index:tap_index + spec_dev...]
    convert_element_type x3 -> x0, local copies, waits for them, and re-layouts: 7.36 us -> none  [the longest x1 4.67 us: shards(): tap_win = (window[tap_index] * extended[:, tap_index:tap_index + spec_dev...]
    all_to_all x1 -> x0, starting transfers between devices: 7.28 us -> none  [shards(): lax.all_to_all((result * inv_root).astype(jnp.bfloat16).reshape(band_coun...]
    all_to_all x1 -> x0, waiting for transfers between devices: 6.51 us -> none  [shards(): lax.all_to_all((result * inv_root).astype(jnp.bfloat16).reshape(band_coun...]
    dot_general x4 -> x0, matrix products: 5.63 us -> none  [table_product(): lax.dot_general(table_rows, windowed_rows, (((1,), (1,)), ((), ())), pref...]
    all_gather x1 -> x0, blocking collectives: 5.48 us -> none  [shards(): shard_piece = lax.all_gather(channel_major, 'quarter', axis=2, tiled=True)]
    reshape x3 -> x0, local copies, waits for them, and re-layouts: 3.75 us -> none  [the longest x1 3.58 us: shards(): (voltages * keep_mask[:, None, None]).reshape(device_signals, spec_dev, F...]
  transfers between devices with their start and end apart: 2 -> 0, of which waited for: 1 -> 0; matrix products, arithmetic and copies ran while one was open for 26% -> 0% of each run, Pallas kernels for 0% -> 0%
where the time goes in v1:
time: 16.7 us; the launch traced here: 16.5 us
  Pallas kernels  15.1 us (90%)
  local copies, waits for them, and re-layouts  1.32 us (8%)
    pallas_call x1, Pallas kernels, shards(): pl.pallas_call(functools.partial(kernel, bands, quarters, ants, pols, spe...  15.1 us
    unnamed x1, local copies, waits for them, and re-layouts  1.32 us

profile of v1, /device:TPU:0, one launch (start us, length us, event | category | flops | bytes accessed | tf_op | source)
XLA Modules:
  0.0 16.5 jit_solution(11464297785028031384)
XLA Ops:
  0.0 15.1 %shard_map.46 = bf16[2,2,16,64]{3,2,1,0:T(8,128)(2,1)} custom-call(s32[4]{0:T(128)} %flag_ref.1, s32[1,32]{1,0:T(1,128)} %bitcast.7, bf16[64,128,128]{2,1,0:T(8,128)(2,1)} %bitcast.6, bf16[8,128,1024]{2,1,0:T(8,128)(2,1)} %constant.2.clone.w_ref), custom_call_target="tpu_custom_call" | custom-call | tf_op jit(solution)/shard_map/pallas_call | solution.py:190
  15.1 1.3 %copy.7 = bf16[2,2,16,64]{3,2,1,0:T(8,128)(2,1)} copy(bf16[2,2,16,64]{3,2,1,0:T(8,128)(2,1)} %shard_map.46) | data formatting | bytes 16384

commit v2 on v1

--- a/solution.py
+++ b/solution.py
@@ -33,8 +33,8 @@
     return np.ascontiguousarray(both.transpose(1, 0, 2)).astype(ml_dtypes.bfloat16)
 
 
-def kernel(bands, quarters, ants, pols, spec, flag_ref, look_ref, x_ref, w_ref, out_ref,
-           xb, wb, xf, sf, send, recv, rf, x_sem, w_sem, own_sem, send_sem, recv_sem):
+def kernel(bands, quarters, ants, pols, spec, flag_in, look_in, x_ref, w_ref, out_ref,
+           flag_ref, look_ref, xb, wb, xf, sf, send, recv, rf, x_sem, w_sem, flag_sem, look_sem, own_sem, send_sem, recv_sem):
     count = bands * quarters
     parts = 2 * CH_DEV
     my_band, my_quarter = lax.axis_index("band"), lax.axis_index("quarter")
@@ -50,6 +50,11 @@
     for g in range(CHUNKS):
         x_copy(g).start()
         w_copy(g).start()
+
+    flag_copy = pltpu.make_async_copy(flag_in, flag_ref, flag_sem)
+    look_copy = pltpu.make_async_copy(look_in, look_ref, look_sem)
+    flag_copy.start()
+    look_copy.start()
 
     barrier = pltpu.get_barrier_semaphore()
 
@@ -82,6 +87,7 @@
     lane = lax.broadcasted_iota(jnp.int32, (1, columns), 1)
     spot = lane % spec
     ant = (lane // spec) % ants
+    flag_copy.wait()
     keep = jnp.zeros((1, columns), jnp.float32)
     for a in range(ants):
         keep = jnp.where(ant == a, (1 - flag_ref[a]).astype(jnp.float32), keep)
@@ -116,6 +122,7 @@
 
     signals = bands * ants * pols
     antennas = bands * ants
+    look_copy.wait()
     look = look_ref[...].astype(jnp.float32)
     out_rows = signals // quarters
 
@@ -187,17 +194,20 @@
     parts = 2 * CH_DEV
     count = bands * quarters
     group = TAPS * parts * bands
+    room = 2 * table.size + 8 * columns * FRAME + 24 * count * parts * columns + 16 * 1024 * 1024
     return pl.pallas_call(
         functools.partial(kernel, bands, quarters, ants, pols, spec),
         out_shape=jax.ShapeDtypeStruct((2, CH_DEV, signals // quarters, signals), jnp.bfloat16),
         in_specs=[
-            pl.BlockSpec(memory_space=pltpu.SMEM),
-            pl.BlockSpec(memory_space=pltpu.VMEM),
-            pl.BlockSpec(memory_space=pl.ANY),
-            pl.BlockSpec(memory_space=pl.ANY),
+            pl.BlockSpec(memory_space=pltpu.HBM),
+            pl.BlockSpec(memory_space=pltpu.HBM),
+            pl.BlockSpec(memory_space=pltpu.HBM),
+            pl.BlockSpec(memory_space=pltpu.HBM),
         ],
         out_specs=pl.BlockSpec(memory_space=pltpu.VMEM),
         scratch_shapes=[
+            pltpu.SMEM((ants,), jnp.int32),
+            pltpu.VMEM((1, bands * ants), jnp.int32),
             pltpu.VMEM((CHUNKS, rows, steps * pols // CHUNKS, LANES), jnp.bfloat16),
             pltpu.VMEM((CHUNKS, group, FRAME // CHUNKS), jnp.bfloat16),
             pltpu.VMEM((rows * steps * pols // CHUNKS, LANES), jnp.float32),
@@ -208,12 +218,14 @@
             pltpu.SemaphoreType.DMA((CHUNKS,)),
             pltpu.SemaphoreType.DMA((CHUNKS,)),
             pltpu.SemaphoreType.DMA,
+            pltpu.SemaphoreType.DMA,
+            pltpu.SemaphoreType.DMA,
             pltpu.SemaphoreType.DMA((count,)),
             pltpu.SemaphoreType.DMA((count,)),
         ],
         compiler_params=pltpu.CompilerParams(
-            collective_id=0, has_side_effects=True, vmem_limit_bytes=63 * 1024 * 1024),
-    )(flagged, lookup.reshape(1, -1), x, jnp.asarray(table))
+            collective_id=0, has_side_effects=True, vmem_limit_bytes=min(room, 63 * 1024 * 1024)),
+    )(*[pltpu.with_memory_space_constraint(v, pltpu.HBM) for v in (flagged, lookup.reshape(1, -1), x, jnp.asarray(table))])
 
 
 def solution(mesh):

time: 16.7 us -> 14.7 us (0.88)
  Pallas kernels: 15.1 us -> 13.9 us
  local copies, waits for them, and re-layouts: 1.32 us -> 0.61 us
    pallas_call x1, Pallas kernels: 15.1 us -> 13.9 us  [shards(): pl.pallas_call(functools.partial(kernel, bands, quarters, ants, pols, spe...]
    unnamed x1, local copies, waits for them, and re-layouts: 1.32 us -> 0.61 us
where the time goes in v2:
time: 14.7 us; the launch traced here: 14.5 us
  Pallas kernels  13.9 us (95%)
  local copies, waits for them, and re-layouts  0.61 us (4%)
    pallas_call x1, Pallas kernels, shards(): pl.pallas_call(functools.partial(kernel, bands, quarters, ants, pols, spe...  13.9 us
    unnamed x1, local copies, waits for them, and re-layouts  0.61 us

profile of v2, /device:TPU:0, one launch (start us, length us, event | category | flops | bytes accessed | tf_op | source)
XLA Modules:
  0.0 14.5 jit_solution(8864045161985167145)
XLA Ops:
  0.0 13.9 %shard_map.46 = bf16[2,2,16,64]{3,2,1,0:T(8,128)(2,1)S(1)} custom-call(s32[4]{0:T(128)} %flag_in.1, s32[1,32]{1,0:T(1,128)} %bitcast.7, bf16[64,128,128]{2,1,0:T(8,128)(2,1)} %bitcast.6, bf16[8,128,1024]{2,1,0:T(8,128)(2,1)} %constant.2.clone.w_ref), custom_call_target="tpu_custom_call" | custom-call | tf_op jit(solution)/shard_map/pallas_call | solution.py:198
  13.9 0.6 %copy.7 = bf16[2,2,16,64]{3,2,1,0:T(8,128)(2,1)} copy(bf16[2,2,16,64]{3,2,1,0:T(8,128)(2,1)S(1)} %shard_map.46) | data formatting | bytes 16384

commit v3 on v2

--- a/solution.py
+++ b/solution.py
@@ -72,11 +72,13 @@
     for g in range(CHUNKS):
         x_copy(g).wait()
         w_copy(g).wait()
-        xf[...] = xb[g].astype(jnp.float32).reshape(rows * pols * wide, LANES)
+        spread = pols * wide + 8
+        for row in range(rows):
+            xf[row * spread:row * spread + pols * wide, :] = xb[g, row].astype(jnp.float32)
         pieces = []
         for j in range(wide):
             pieces.append(jnp.concatenate(
-                [xf[pl.ds(pols * j + p, rows, stride=pols * wide), :] for p in range(pols)], axis=0
+                [xf[pl.ds(pols * j + p, rows, stride=spread), :] for p in range(pols)], axis=0
             ).astype(jnp.bfloat16))
         block = jnp.concatenate(pieces, axis=1)
         part = lax.dot_general(wb[g], block, (((1,), (1,)), ((), ())), preferred_element_type=jnp.float32)
@@ -210,7 +212,7 @@
             pltpu.VMEM((1, bands * ants), jnp.int32),
             pltpu.VMEM((CHUNKS, rows, steps * pols // CHUNKS, LANES), jnp.bfloat16),
             pltpu.VMEM((CHUNKS, group, FRAME // CHUNKS), jnp.bfloat16),
-            pltpu.VMEM((rows * steps * pols // CHUNKS, LANES), jnp.float32),
+            pltpu.VMEM((rows * (steps * pols // CHUNKS + 8), LANES), jnp.float32),
             pltpu.VMEM((bands * 2 * parts, columns), jnp.float32),
             pltpu.VMEM((bands, 2 * parts, columns), jnp.bfloat16),
             pltpu.VMEM((count, 2 * parts, columns), jnp.bfloat16),

time: 14.7 us -> 14.3 us (0.973)
  Pallas kernels: 13.9 us -> 13.6 us
    pallas_call x1, Pallas kernels: 13.9 us -> 13.6 us  [shards(): pl.pallas_call(functools.partial(kernel, bands, quarters, ants, pols, spe...]
where the time goes in v3:
time: 14.3 us; the launch traced here: 14.2 us
  Pallas kernels  13.6 us (95%)
  local copies, waits for them, and re-layouts  0.61 us (4%)
    pallas_call x1, Pallas kernels, shards(): pl.pallas_call(functools.partial(kernel, bands, quarters, ants, pols, spe...  13.6 us
    unnamed x1, local copies, waits for them, and re-layouts  0.61 us

profile of v3, /device:TPU:0, one launch (start us, length us, event | category | flops | bytes accessed | tf_op | source)
XLA Modules:
  0.0 14.2 jit_solution(2638228817811384531)
XLA Ops:
  0.0 13.6 %shard_map.46 = bf16[2,2,16,64]{3,2,1,0:T(8,128)(2,1)S(1)} custom-call(s32[4]{0:T(128)} %flag_in.1, s32[1,32]{1,0:T(1,128)} %bitcast.7, bf16[64,128,128]{2,1,0:T(8,128)(2,1)} %bitcast.6, bf16[8,128,1024]{2,1,0:T(8,128)(2,1)} %constant.2.clone.w_ref), custom_call_target="tpu_custom_call" | custom-call | tf_op jit(solution)/shard_map/pallas_call | solution.py:200
  13.6 0.6 %copy.7 = bf16[2,2,16,64]{3,2,1,0:T(8,128)(2,1)} copy(bf16[2,2,16,64]{3,2,1,0:T(8,128)(2,1)S(1)} %shard_map.46) | data formatting | bytes 16384
